TPU v7x, 128 devices: a whole 4x4x4 slice. The times are simulated.
128 devices in a mesh: space: 32 (over x, y, core), head: 4 (over z).
Axes of the slice: x: 4, y: 4, z: 4, core: 2. Of those that a mesh axis runs over, the one named last changes fastest.
Arguments:
- snapshot: bfloat16 [32768, 1536], P('space'), may hold values from -6 to 6
- norm_gain: float32 [1536], replicated, may hold values from 0.25 to 1.75
- w_query: bfloat16 [1536, 1536], P(None, 'head'), may hold values from -0.15625 to 0.15625
- w_key: bfloat16 [1536, 1536], P(None, 'head'), may hold values from -0.15625 to 0.15625
- w_value: bfloat16 [1536, 1536], P(None, 'head'), may hold values from -0.15625 to 0.15625
- w_out: bfloat16 [1536, 1536], P('head'), may hold values from -0.15625 to 0.15625
- cache_key: bfloat16 [8, 32768, 1536], P(None, 'space', 'head'), may hold values from -420 to 420
- cache_value: bfloat16 [8, 32768, 1536], P(None, 'space', 'head'), may hold values from -6 to 6
- pattern: int32 [256, 8], P('space'), may hold values from 0 to 255, as said below
- counts: int32 [256], P('space'), may hold values from 1 to 8, as said below
Outputs:
- rolled: bfloat16 [32768, 1536], P('space')
Inputs may be any that keep to these rules, and one draw needn't show every extreme that they name: `pattern`: each index is a block within 12 blocks of its query block, counted periodically over the 256 blocks; the 8 entries of one query block are distinct. `counts`: loads are uneven; some query block has all 8 slots live.
All inputs are finite; a program needn't handle non-finite values.
Results may differ from a plain program's by a relative error of at most 0.014.
Values may be sent and summed in bfloat16 or wider, within the bound.
A program may use at most 192 MiB of HBM per device.

v0:
```python
import jax
import jax.numpy as jnp
from jax import lax
from jax.sharding import PartitionSpec as P

HD = 128
BLK = 128
MAXK = 8
FRAMES = 8
STEPS = 2


def shifted_2(value, axis, steps):
    count = lax.axis_size(axis)
    pairs = [(source, (source + steps) % count) for source in range(count)]
    return lax.ppermute(value, axis, pairs)


def on_device(
    snapshot, norm_gain, w_query, w_key, w_value, w_out, cache_key, cache_value, pattern, counts
):
    tok_rows = snapshot.shape[0]
    blocks = tok_rows // BLK
    reach_blocks = blocks + blocks // 2
    block_count_total = blocks * lax.axis_size("space")
    first_block = lax.axis_index("space") * blocks
    local_width = w_query.shape[1]
    heads_here = local_width // HD
    inv_scale = 1.0 / HD**0.5
    own_block = first_block + jnp.arange(blocks, dtype=jnp.int32)
    relative = (
        pattern - own_block[:, None] + block_count_total // 2
    ) % block_count_total - block_count_total // 2
    where_block = (jnp.arange(blocks, dtype=jnp.int32)[:, None] + reach_blocks + relative).reshape(
        blocks * MAXK
    )
    live_slot = jnp.arange(MAXK, dtype=jnp.int32)[None, :] < counts[:, None]
    live_keys = jnp.repeat(live_slot, BLK, axis=1)[:, None, :]
    state = snapshot
    key_frames = [cache_key[frame].reshape(blocks, BLK, local_width) for frame in range(FRAMES)]
    value_frames = [cache_value[frame].reshape(blocks, BLK, local_width) for frame in range(FRAMES)]
    for rollout in range(STEPS):
        state_wide = state.astype(jnp.float32)
        meansq = jnp.mean(state_wide * state_wide, axis=-1, keepdims=True)
        normed = (state_wide * lax.rsqrt(meansq + 1e-05) * norm_gain).astype(jnp.bfloat16)
        queries = jnp.dot(normed, w_query, preferred_element_type=jnp.float32).astype(jnp.bfloat16)
        key_new = jnp.dot(normed, w_key, preferred_element_type=jnp.float32).astype(jnp.bfloat16)
        value_new = jnp.dot(normed, w_value, preferred_element_type=jnp.float32).astype(
            jnp.bfloat16
        )
        key_value = jnp.stack([key_new, value_new])
        shifted = {}
        for stride in (2, 1, -1, -2):
            shifted[stride] = shifted_2(key_value, "space", stride)
        window = jnp.concatenate(
            [shifted[2], shifted[1], key_value, shifted[-1], shifted[-2]], axis=1
        )
        cut_rows = (2 * blocks - reach_blocks) * BLK
        window = window[:, cut_rows : cut_rows + (blocks + 2 * reach_blocks) * BLK]
        window = window.reshape(2, blocks + 2 * reach_blocks, BLK, local_width)
        taken = jnp.take(window, where_block, axis=1).reshape(2, blocks, MAXK * BLK, local_width)
        block_query = queries.reshape(blocks, BLK, local_width)
        head_outputs = []
        for head in range(heads_here):
            low = head * HD
            high = low + HD
            per_head_query = block_query[:, :, low:high]
            per_head_key = taken[0, :, :, low:high]
            per_head_value = taken[1, :, :, low:high]
            spatial = (
                jnp.einsum(
                    "hcj,hmj->hcm", per_head_query, per_head_key, preferred_element_type=jnp.float32
                )
                * inv_scale
            )
            spatial = jnp.where(live_keys, spatial, jnp.float32(-1e30))
            temporal = [
                jnp.einsum(
                    "urt,urt->ur",
                    per_head_query,
                    key_frames[frame][:, :, low:high],
                    preferred_element_type=jnp.float32,
                )
                * inv_scale
                for frame in range(FRAMES)
            ]
            top_score = spatial.max(axis=2)
            for frame in range(FRAMES):
                top_score = jnp.maximum(top_score, temporal[frame])
            spatial_exponent = jnp.exp(spatial - top_score[..., None])
            temporal_exp = [jnp.exp(temporal[frame] - top_score) for frame in range(FRAMES)]
            total = spatial_exponent.sum(axis=2)
            for frame in range(FRAMES):
                total = total + temporal_exp[frame]
            spatial_attention_weight = (spatial_exponent / total[..., None]).astype(jnp.bfloat16)
            mixed = jnp.einsum(
                "iwe,iea->iwa",
                spatial_attention_weight,
                per_head_value,
                preferred_element_type=jnp.float32,
            )
            for frame in range(FRAMES):
                temporal_weight = (temporal_exp[frame] / total).astype(jnp.bfloat16)
                mixed = mixed + temporal_weight.astype(jnp.float32)[..., None] * value_frames[
                    frame
                ][:, :, low:high].astype(jnp.float32)
            head_outputs.append(mixed.astype(jnp.bfloat16))
        attended_output = jnp.concatenate(head_outputs, axis=2).reshape(tok_rows, local_width)
        out_term = jnp.dot(attended_output, w_out, preferred_element_type=jnp.float32)
        update = lax.psum(out_term.astype(jnp.bfloat16), "head").astype(jnp.float32)
        state = (state_wide + update).astype(jnp.bfloat16)
        if rollout + 1 < STEPS:
            key_frames = key_frames[1:] + [key_new.reshape(blocks, BLK, local_width)]
            value_frames = value_frames[1:] + [value_new.reshape(blocks, BLK, local_width)]
    return state


def solution(mesh):
    placed = (
        P("space", None),
        P(),
        P(None, "head"),
        P(None, "head"),
        P(None, "head"),
        P("head", None),
        P(None, "space", "head"),
        P(None, "space", "head"),
        P("space", None),
        P("space"),
    )
    return jax.shard_map(
        on_device, mesh=mesh, in_specs=placed, out_specs=P("space", None), check_vma=False
    )
```

profile of v0, /device:TPU:1, one launch (start us, length us, event | category | flops | bytes accessed | tf_op | source)
XLA Modules:
  0.0 427.5 jit_solution(5075904005685580996)
XLA Ops:
  9.3 4.2 convolution_convert_fusion.6
  16.8 5.8 %collective-permute-start.3 = (bf16[2,1024,384]{2,1,0:T(8,128)(2,1)}, bf16[2,1024,384]{2,1,0:T(8,128)(2,1)}, u32[]{:S(2)}, u32[]{:S(2)}) collective-permute-start(bf16[2,1024,384]{2,1,0:T(8,128)(2,1)} %pad_maximum_fusion), channel_id=1, source_target_pairs={{0,120},{4,124},{8,0},{12,4},{16,8},{20,12},{24,16},{28,20},{32,24... | collective-permute-start | bytes 4718600 | tf_op jit(solution)/shard_map/ppermute | solution.py:16
  24.7 3.9 convolution_convert_fusion.7
  28.6 5.0 %fusion.215 = (bf16[1,1024,384]{2,1,0:T(8,128)(2,1)S(1)}, bf16[1,1024,384]{2,1,0:T(8,128)(2,1)}, bf16[1,1024,384]{2,1,0:T(8,128)(2,1)}, bf16[1,1024,384]{2,1,0:T...) fusion(bf16[8,1024,384]{2,1,0:T(8,128)(2,1)} %param.18), kind=kLoop, calls=%fused_computation.484 | loop fusion | bytes 12582912 | tf_op jit(solution)/shard_map/slice | solution.py:40
  88.0 3.3 fusion.94
  91.3 3.4 fusion.95
  102.2 3.2 slice.407
  105.5 10.7 %gather_fusion = bf16[64,2,128,384]{3,2,1,0:T(8,128)(2,1)} fusion(bf16[2,32,128,384]{3,2,1,0:T(8,128)(2,1)} %bitcast.204, s32[1024]{0:T(1024)} %pad_clamp_fusion), kind=kCustom, calls=%fused_computation.clone | custom fusion | bytes 25166080 | tf_op jit(solution)/shard_map/jit(_take)/gather | solution.py:61
  116.1 6.9 %select_bitcast_fusion.1 = bf16[2,64,128,384]{3,2,0,1:T(8,128)(2,1)S(1)} fusion(bf16[64,2,128,384]{3,2,1,0:T(8,128)(2,1)} %gather_fusion, pred[64]{0:T(512)(128)(4,1)} %compare_and_fusion), kind=kLoop, calls=%fused_computation.3 | loop fusion | flops 6291456 | bytes 25165888 | tf_op jit(solution)/shard_map/jit(_take)/select_n | solution.py:61
  123.1 3.3 copy.22
  141.6 4.6 %convolution_convert_fusion.1 = bf16[1024,1536]{1,0:T(8,128)(2,1)} fusion(bf16[1024,384]{1,0:T(8,128)(2,1)} %bitcast.260, bf16[384,1536]{1,0:T(8,128)(2,1)S(1)} %copy-done), kind=kOutput, calls=%fused_computation.37 | convolution fusion | flops 1209532416 | bytes 5111808 | tf_op jit(solution)/shard_map/dot_general | solution.py:109
  146.5 77.3 %all-reduce.3.cloned.1.call-done = bf16[1024,1536]{1,0:T(8,128)(2,1)} async-done(((bf16[1024,1536]{1,0:T(8,128)(2,1)}), bf16[1024,1536]{1,0:T(8,128)(2,1)}) %all-reduce.3.cloned.1.call-update) | async-done | bytes 3145744 | tf_op jit(solution)/shard_map/psum | solution.py:110
  223.7 4.1 fusion.4
  241.3 3.6 collective-permute-start.7
  244.9 4.0 convolution_convert_fusion.4
  254.3 19.5 %collective-permute-done.4 = bf16[2,1024,384]{2,1,0:T(8,128)(2,1)} collective-permute-done((bf16[2,1024,384]{2,1,0:T(8,128)(2,1)}, bf16[2,1024,384]{2,1,0:T(8,128)(2,1)}, u32[]{:S(2)}, u32[]{:S(2)}) %collective-permute-start.4) | collective-permute-done | bytes 1572896 | tf_op jit(solution)/shard_map/ppermute | solution.py:16
  275.4 12.3 %collective-permute-done.5 = bf16[2,1024,384]{2,1,0:T(8,128)(2,1)} collective-permute-done((bf16[2,1024,384]{2,1,0:T(8,128)(2,1)}, bf16[2,1024,384]{2,1,0:T(8,128)(2,1)}, u32[]{:S(2)}, u32[]{:S(2)}) %collective-permute-start.5) | collective-permute-done | bytes 1572896 | tf_op jit(solution)/shard_map/ppermute | solution.py:16
  289.7 4.2 collective-permute-done.6
  297.8 10.9 %gather_fusion.1 = bf16[64,2,128,384]{3,2,1,0:T(8,128)(2,1)} fusion(bf16[2,32,128,384]{3,2,1,0:T(8,128)(2,1)} %bitcast.203, s32[1024]{0:T(1024)} %pad_clamp_fusion), kind=kCustom, calls=%fused_computation.1.clone | custom fusion | bytes 25166080 | tf_op jit(solution)/shard_map/jit(_take)/gather | solution.py:61
  308.7 7.0 %select_bitcast_fusion = bf16[2,64,128,384]{3,2,0,1:T(8,128)(2,1)S(1)} fusion(bf16[64,2,128,384]{3,2,1,0:T(8,128)(2,1)} %gather_fusion.1, pred[64]{0:T(512)(128)(4,1)S(1)} %copy-done.117), kind=kLoop, calls=%fused_computation.2 | loop fusion | flops 6291456 | bytes 25165888 | tf_op jit(solution)/shard_map/jit(_take)/select_n | solution.py:61
  315.7 3.3 copy.51
  333.4 3.5 convolution_convert_fusion
  336.9 76.8 %all-reduce.5.cloned.1.call-done = bf16[1024,1536]{1,0:T(8,128)(2,1)} async-done(((bf16[1024,1536]{1,0:T(8,128)(2,1)}), bf16[1024,1536]{1,0:T(8,128)(2,1)}) %all-reduce.5.cloned.1.call-update) | async-done | bytes 3145744 | tf_op jit(solution)/shard_map/psum | solution.py:110
  413.7 6.7 %fusion.7 = bf16[1024,1536]{1,0:T(8,128)(2,1)} fusion(bf16[1024,1536]{1,0:T(8,128)(2,1)} %all-reduce.5.cloned.1.call-done, bf16[1024,1536]{1,0:T(8,128)(2,1)} %all-reduce.3.cloned.1.call-done, bf16[1024,1536]{1,0:T(8,128)(2,1)} %param.12), kind=kLoop, calls=%fused_computation.17 | loop fusion | flops 12582912 | bytes 12582912 | tf_op jit(solution)/shard_map/convert_element_type | solution.py:111
  (371 shorter events, 124.2 us)
Async XLA Ops:
  6.5 135.1 %copy-start = (bf16[384,1536]{1,0:T(8,128)(2,1)S(1)}, bf16[384,1536]{1,0:T(8,128)(2,1)}, u32[]{:S(2)}) copy-start(bf16[384,1536]{1,0:T(8,128)(2,1)} %param.17) | copy-start | bytes 3538948
  6.5 217.2 %all-reduce.3.cloned.1.call-start = ((), (), s32[]{:S(2)}) async-start(), calls=%async_computation | async-start | bytes 6291456 | tf_op jit(solution)/shard_map/psum | solution.py:110
  13.5 11.0 %copy-start.116 = (s32[8,8]{1,0:T(8,128)S(1)}, s32[8,8]{1,0:T(8,128)}, u32[]{:S(2)}) copy-start(s32[8,8]{1,0:T(8,128)} %param.20) | copy-start | bytes 772
  13.5 11.1 %copy-start.121 = (bf16[1536,384]{1,0:T(8,128)(2,1)S(1)}, bf16[1536,384]{1,0:T(8,128)(2,1)}, u32[]{:S(2)}) copy-start(bf16[1536,384]{1,0:T(8,128)(2,1)} %param.14) | copy-start | bytes 3538948
  16.8 83.7 %collective-permute-start.3 = (bf16[2,1024,384]{2,1,0:T(8,128)(2,1)}, bf16[2,1024,384]{2,1,0:T(8,128)(2,1)}, u32[]{:S(2)}, u32[]{:S(2)}) collective-permute-start(bf16[2,1024,384]{2,1,0:T(8,128)(2,1)} %pad_maximum_fusion), channel_id=1, source_target_pairs={{0,120},{4,124},{8,0},{12,4},{16,8},{20,12},{24,16},{28,20},{32,24... | collective-permute-start | bytes 4718600 | tf_op jit(solution)/shard_map/ppermute | solution.py:16
  22.6 75.8 %collective-permute-start.2 = (bf16[2,1024,384]{2,1,0:T(8,128)(2,1)}, bf16[2,1024,384]{2,1,0:T(8,128)(2,1)}, u32[]{:S(2)}, u32[]{:S(2)}) collective-permute-start(bf16[2,1024,384]{2,1,0:T(8,128)(2,1)} %pad_maximum_fusion), channel_id=1, source_target_pairs={{0,124},{4,0},{8,4},{12,8},{16,12},{20,16},{24,20},{28,24},{32,28}... | collective-permute-start | bytes 4718600 | tf_op jit(solution)/shard_map/ppermute | solution.py:16
  23.5 72.8 %collective-permute-start.1 = (bf16[2,1024,384]{2,1,0:T(8,128)(2,1)}, bf16[2,1024,384]{2,1,0:T(8,128)(2,1)}, u32[]{:S(2)}, u32[]{:S(2)}) collective-permute-start(bf16[2,1024,384]{2,1,0:T(8,128)(2,1)} %pad_maximum_fusion), channel_id=1, source_target_pairs={{0,4},{4,8},{8,12},{12,16},{16,20},{20,24},{24,28},{28,32},{32,36}... | collective-permute-start | bytes 4718600 | tf_op jit(solution)/shard_map/ppermute | solution.py:16
  24.3 70.4 %collective-permute-start = (bf16[2,1024,384]{2,1,0:T(8,128)(2,1)}, bf16[2,1024,384]{2,1,0:T(8,128)(2,1)}, u32[]{:S(2)}, u32[]{:S(2)}) collective-permute-start(bf16[2,1024,384]{2,1,0:T(8,128)(2,1)} %pad_maximum_fusion), channel_id=1, source_target_pairs={{0,8},{4,12},{8,16},{12,20},{16,24},{20,28},{24,32},{28,36},{32,40... | collective-permute-start | bytes 4718600 | tf_op jit(solution)/shard_map/ppermute | solution.py:16
  24.7 9.0 %slice-start = ((s8[6291456]{0:T(1024)(128)(4,1)}), s8[4194304]{0:T(1024)(128)(4,1)S(1)}, s32[]{:S(2)}) async-start(s8[6291456]{0:T(1024)(128)(4,1)} %bitcast.249), calls=%async_computation.2 | async-start | bytes 8388608
  33.6 9.1 %copy-start.5 = (bf16[1,1024,384]{2,1,0:T(8,128)(2,1)}, bf16[1,1024,384]{2,1,0:T(8,128)(2,1)S(1)}, u32[]{:S(2)}) copy-start(bf16[1,1024,384]{2,1,0:T(8,128)(2,1)S(1)} %get-tuple-element.117) | copy-start | bytes 2359300
  33.7 9.1 %copy-start.8 = (bf16[1,1024,384]{2,1,0:T(8,128)(2,1)}, bf16[1,1024,384]{2,1,0:T(8,128)(2,1)S(1)}, u32[]{:S(2)}) copy-start(bf16[1,1024,384]{2,1,0:T(8,128)(2,1)S(1)} %get-tuple-element.114) | copy-start | bytes 2359300
  59.2 28.7 %copy-start.122 = (s32[8]{0:T(128)S(1)}, s32[8]{0:T(128)}, u32[]{:S(2)}) copy-start(s32[8]{0:T(128)} %param.21) | copy-start | bytes 100
  146.2 81.6 %copy-start.115 = (f32[1536]{0:T(1024)S(1)}, f32[1536]{0:T(1024)}, u32[]{:S(2)}) copy-start(f32[1536]{0:T(1024)} %param.13) | copy-start | bytes 18436
  146.2 267.5 %all-reduce.5.cloned.1.call-start = ((), (), s32[]{:S(2)}) async-start(), calls=%async_computation.1 | async-start | bytes 6291456 | tf_op jit(solution)/shard_map/psum | solution.py:110
  235.1 38.8 %collective-permute-start.4 = (bf16[2,1024,384]{2,1,0:T(8,128)(2,1)}, bf16[2,1024,384]{2,1,0:T(8,128)(2,1)}, u32[]{:S(2)}, u32[]{:S(2)}) collective-permute-start(bf16[2,1024,384]{2,1,0:T(8,128)(2,1)} %pad_maximum_fusion.1), channel_id=1, source_target_pairs={{0,8},{4,12},{8,16},{12,20},{16,24},{20,28},{24,32},{28,36},{32,40... | collective-permute-start | bytes 4718600 | tf_op jit(solution)/shard_map/ppermute | solution.py:16
  236.3 51.4 %collective-permute-start.5 = (bf16[2,1024,384]{2,1,0:T(8,128)(2,1)}, bf16[2,1024,384]{2,1,0:T(8,128)(2,1)}, u32[]{:S(2)}, u32[]{:S(2)}) collective-permute-start(bf16[2,1024,384]{2,1,0:T(8,128)(2,1)} %pad_maximum_fusion.1), channel_id=1, source_target_pairs={{0,4},{4,8},{8,12},{12,16},{16,20},{20,24},{24,28},{28,32},{32,36}... | collective-permute-start | bytes 4718600 | tf_op jit(solution)/shard_map/ppermute | solution.py:16
  241.3 9.2 %copy-start.4 = (bf16[1,1024,384]{2,1,0:T(8,128)(2,1)S(1)}, bf16[1,1024,384]{2,1,0:T(8,128)(2,1)}, u32[]{:S(2)}) copy-start(bf16[1,1024,384]{2,1,0:T(8,128)(2,1)} %get-tuple-element.115) | copy-start | bytes 2359300
  241.3 9.2 %copy-start.6 = (bf16[1,1024,384]{2,1,0:T(8,128)(2,1)S(1)}, bf16[1,1024,384]{2,1,0:T(8,128)(2,1)}, u32[]{:S(2)}) copy-start(bf16[1,1024,384]{2,1,0:T(8,128)(2,1)} %copy-done.5) | copy-start | bytes 2359300
  241.3 9.2 %copy-start.7 = (bf16[1,1024,384]{2,1,0:T(8,128)(2,1)S(1)}, bf16[1,1024,384]{2,1,0:T(8,128)(2,1)}, u32[]{:S(2)}) copy-start(bf16[1,1024,384]{2,1,0:T(8,128)(2,1)} %get-tuple-element.121) | copy-start | bytes 2359300
  241.3 52.9 %collective-permute-start.7 = (bf16[2,1024,384]{2,1,0:T(8,128)(2,1)}, bf16[2,1024,384]{2,1,0:T(8,128)(2,1)S(1)}, u32[]{:S(2)}, u32[]{:S(2)}) collective-permute-start(bf16[2,1024,384]{2,1,0:T(8,128)(2,1)} %pad_maximum_fusion.1), channel_id=1, source_target_pairs={{0,120},{4,124},{8,0},{12,4},{16,8},{20,12},{24,16},{28,20},{32,24... | collective-permute-start | bytes 4718600 | tf_op jit(solution)/shard_map/ppermute | solution.py:16
  244.9 49.0 %collective-permute-start.6 = (bf16[2,1024,384]{2,1,0:T(8,128)(2,1)}, bf16[2,1024,384]{2,1,0:T(8,128)(2,1)S(1)}, u32[]{:S(2)}, u32[]{:S(2)}) collective-permute-start(bf16[2,1024,384]{2,1,0:T(8,128)(2,1)} %pad_maximum_fusion.1), channel_id=1, source_target_pairs={{0,124},{4,0},{8,4},{12,8},{16,12},{20,16},{24,20},{28,24},{32,28}... | collective-permute-start | bytes 4718600 | tf_op jit(solution)/shard_map/ppermute | solution.py:16
  252.4 37.0 %copy-start.19 = (bf16[1,1024,384]{2,1,0:T(8,128)(2,1)S(1)}, bf16[1,1024,384]{2,1,0:T(8,128)(2,1)}, u32[]{:S(2)}) copy-start(bf16[1,1024,384]{2,1,0:T(8,128)(2,1)} %copy-done.18) | copy-start | bytes 2359300
  252.4 37.0 %copy-start.21 = (bf16[1,1024,384]{2,1,0:T(8,128)(2,1)S(1)}, bf16[1,1024,384]{2,1,0:T(8,128)(2,1)}, u32[]{:S(2)}) copy-start(bf16[1,1024,384]{2,1,0:T(8,128)(2,1)} %copy-done.20) | copy-start | bytes 2359300
  297.8 10.9 %copy-start.117 = (pred[64]{0:T(512)(128)(4,1)S(1)}, pred[64]{0:T(512)(128)(4,1)}, u32[]{:S(2)}) copy-start(pred[64]{0:T(512)(128)(4,1)} %compare_and_fusion) | copy-start | bytes 196
  (111 other events, 290.1 us)
Sparse Core Ops, SparseCore 0:
  146.4 77.3 all-reduce.2
  337.0 76.6 all-reduce.4
where the time goes:
time: 433 us; the launch traced here: 427 us
  waiting for transfers between devices  190 us (44%)
  local copies, waits for them, and re-layouts  108 us (25%)
  other arithmetic  51.5 us (12%)
  matrix products  46.7 us (11%)
  between operations  15.8 us (4%)
  starting transfers between devices  14.9 us (3%)
    psum x2, waiting for transfers between devices, on_device(): update = lax.psum(out_term.astype(jnp.bfloat16), 'head').astype(jnp.float32)  154 us
    unnamed x283, local copies, waits for them, and re-layouts  56.2 us
    ppermute x8, waiting for transfers between devices, shifted_2(): return lax.ppermute(value, axis, pairs)  36 us
    gather x2, local copies, waits for them, and re-layouts, on_device(): jnp.take(window, where_block, axis=1)  21.5 us
    ppermute x8, starting transfers between devices, shifted_2(): return lax.ppermute(value, axis, pairs)  14.7 us
    select_n x3, other arithmetic, on_device(): jnp.take(window, where_block, axis=1)  13.9 us
    dot_general x6, other arithmetic, on_device(): jnp.einsum('urt,urt->ur', per_head_query, key_frames[frame][:, :, low:hig...  13.5 us
    dot_general x6, matrix products, on_device(): jnp.einsum('iwe,iea->iwa', spatial_attention_weight, per_head_value, pref...  12.5 us
  transfers between devices with their start and end apart: 10, of which 5 were waited for; matrix products, arithmetic and copies ran while one was open for 21% of the time, Pallas kernels for 0%

commit v1 on v0

v1 whole, which is shorter than its diff:
```python
import functools
import math

import jax
import jax.numpy as jnp
from jax import lax
from jax.experimental import pallas as pl
from jax.experimental.pallas import tpu as pltpu
from jax.sharding import PartitionSpec as P

HD = 128
BLK = 128
MAXK = 8
FRAMES = 8
STEPS = 2
HALO = 12
QBLK = 2
NQ = 4
EPS = 1e-05
MASKED = -1e30
MESH = pl.DeviceIdType.MESH
F32 = jnp.float32
BF16 = jnp.bfloat16
SCALE2 = math.log2(math.e) / math.sqrt(HD)
NORM_ROWS = 32
TIME_ROWS = 32


def kernel(
    n_space, n_head,
    pattern, counts, snapshot, gain, w_query, w_key, w_value, w_out, cache_key, cache_value,
    rolled,
    state, wqkv, wout, ckey, cvalue, kv0, kv1, far, att, queries, normed, top_t, sum_t, acc_t,
    in_sem, w_sem, cache_sem, out_sem,
    near_s, near_r, chip_s, chip_r, far_s, far_r, rel_s, rel_r, ag_s, ag_r, fw_s, fw_r,
    wd_s, wd_r, wf_s, wf_r, wc_s, wc_r,
):
    kv = (kv0, kv1)
    rows, width = state.shape
    lw = w_query.shape[1]
    heads = lw // HD
    blocks = rows // BLK
    total_blocks = blocks * n_space
    qrows = QBLK * BLK
    window = kv0.shape[0]

    space = lax.axis_index("space")
    z = lax.axis_index("head")
    core = lax.rem(space, 2)

    def wrap(s):
        return lax.rem(s + n_space, n_space)

    up = (space, lax.rem(z + 1, n_head))
    down = (space, lax.rem(z + n_head - 1, n_head))
    partner = (space + 1 - 2 * core, z)
    near_dev = (wrap(space - 1 + 2 * core), z)
    far_dev = (wrap(space + 2 - 4 * core), z)
    far_src = (wrap(space - 2 + 4 * core), z)
    z_up = lax.rem(z + 1, n_head)
    z_down = lax.rem(z + n_head - 1, n_head)

    def first_block(q, c):
        return (1 - c) * (blocks - QBLK - QBLK * q) + c * QBLK * q

    def col(group):
        return pl.ds(pl.multiple_of(group * lw, 128), lw)

    def rcopy(src, dst, ssem, rsem, dev):
        return pltpu.make_async_remote_copy(
            src_ref=src, dst_ref=dst, send_sem=ssem, recv_sem=rsem, device_id=dev, device_id_type=MESH
        )

    def near_copy(t, q):
        b = first_block(q, core)
        return rcopy(
            kv[t].at[pl.ds(HALO + b, QBLK)],
            kv[t].at[pl.ds(20 - 16 * core + b, QBLK)],
            near_s.at[t, q], near_r.at[t, q], near_dev,
        )

    def chip_copy(t, q):
        b = first_block(q, core)
        return rcopy(
            kv[t].at[pl.ds(HALO + b, QBLK)],
            kv[t].at[pl.ds(4 + 16 * core + b, QBLK)],
            chip_s.at[t, q], chip_r.at[t, q], partner,
        )

    def far_copy(t, q):
        b = first_block(q, core)
        return rcopy(
            kv[t].at[pl.ds(HALO + b, QBLK)],
            far.at[t, pl.ds(b - 4 * (1 - core), QBLK)],
            far_s.at[t, q], far_r.at[t, q], far_dev,
        )

    def relay_copy(t, q):
        w = 4 + 16 * core + first_block(q, 1 - core)
        return rcopy(
            kv[t].at[pl.ds(w, QBLK)],
            kv[t].at[pl.ds(w - 8 + 16 * core, QBLK)],
            rel_s.at[t, q - 2], rel_r.at[t, q - 2], partner,
        )

    def gather_copy(t, q, d):
        r = pl.multiple_of(first_block(q, core) * BLK, BLK)
        part = att.at[t, pl.ds(r, qrows), col(z)]
        return rcopy(part, part, ag_s.at[t, q, d], ag_r.at[t, q, d], up if d == 0 else down)

    def forward_copy(t, q, d):
        r = pl.multiple_of(first_block(q, core) * BLK + d * (qrows // 2), BLK)
        part = att.at[t, pl.ds(r, qrows // 2), col(z_down if d == 0 else z_up)]
        return rcopy(part, part, fw_s.at[t, q, d], fw_r.at[t, q, d], up if d == 0 else down)

    half = lw // 2

    def w_rows(group, offset, count):
        return wout.at[pl.ds(pl.multiple_of(group * lw + offset, 32), count), :]

    def w_copy(d):
        part = w_rows(z, half * core, half)
        return rcopy(part, part, wd_s.at[d], wd_r.at[d], up if d == 0 else down)

    def w_forward(d):
        part = w_rows(z_down if d == 0 else z_up, half * core + d * (half // 2), half // 2)
        return rcopy(part, part, wf_s.at[d], wf_r.at[d], up if d == 0 else down)

    def w_chip(k):
        part = w_rows(lax.rem(z + 1 + k, n_head), half * core, half)
        return rcopy(part, part, wc_s.at[k], wc_r.at[k], partner)

    def in_copy(q):
        r = pl.multiple_of(first_block(q, core) * BLK, BLK)
        return pltpu.make_async_copy(
            snapshot.at[pl.ds(r, qrows), :], state.at[pl.ds(r, qrows), :], in_sem.at[q]
        )

    def out_copy(q):
        r = pl.multiple_of(first_block(q, core) * BLK, BLK)
        return pltpu.make_async_copy(
            state.at[pl.ds(r, qrows), :], rolled.at[pl.ds(r, qrows), :], out_sem.at[q]
        )

    weight_copies = [
        pltpu.make_async_copy(ref, wqkv.at[:, pl.ds(i * lw, lw)], w_sem.at[i])
        for i, ref in enumerate((w_query, w_key, w_value))
    ]
    w_out_copy = pltpu.make_async_copy(w_out, w_rows(z, 0, lw), w_sem.at[3])
    cache_copies = [
        pltpu.make_async_copy(cache_key, ckey, cache_sem.at[0]),
        pltpu.make_async_copy(cache_value, cvalue, cache_sem.at[1]),
    ]

    def qkv(t, q):
        b = first_block(q, core)
        r0 = b * BLK

        def norm_rows(i, _):
            r = pl.multiple_of(r0 + i * NORM_ROWS, NORM_ROWS)
            wide = state[pl.ds(r, NORM_ROWS), :].astype(F32)
            meansq = jnp.mean(wide * wide, axis=-1, keepdims=True)
            normed[pl.ds(pl.multiple_of(i * NORM_ROWS, NORM_ROWS), NORM_ROWS), :] = (
                wide * lax.rsqrt(meansq + EPS) * gain[...]
            ).astype(BF16)
            return 0

        lax.fori_loop(0, qrows // NORM_ROWS, norm_rows, 0)
        for i in range(2):
            out = jnp.dot(
                normed[...], wqkv[:, lw * (1 + i) : lw * (2 + i)], preferred_element_type=F32
            ).astype(BF16)
            for k in range(QBLK):
                kv[t][HALO + b + k, i] = out[k * BLK : (k + 1) * BLK]
        return r0

    def qkv_queries(q):
        r0 = pl.multiple_of(first_block(q, core) * BLK, BLK)
        queries[pl.ds(r0, qrows), :] = jnp.dot(
            normed[...], wqkv[:, :lw], preferred_element_type=F32
        ).astype(BF16)

    def temporal(t, r, h):
        lanes = slice(h * HD, (h + 1) * HD)
        at = pl.ds(r, TIME_ROWS)
        query = queries[at, lanes].astype(F32)
        b = lax.div(r, BLK)
        inner = pl.ds(pl.multiple_of(lax.rem(r, BLK), TIME_ROWS), TIME_ROWS)
        frames = range(t, FRAMES)
        keys = [ckey[f, at, lanes] for f in frames]
        keys += [kv0[HALO + b, 0, inner, lanes]] * t
        scores = [jnp.sum(query * k.astype(F32), axis=-1, keepdims=True) for k in keys]
        top = functools.reduce(jnp.maximum, scores)
        exps = [jnp.exp2((s - top) * SCALE2) for s in scores]
        values = [cvalue[f, at, lanes] for f in frames]
        values += [kv0[HALO + b, 1, inner, lanes]] * t
        acc = functools.reduce(jnp.add, [e * v.astype(F32) for e, v in zip(exps, values)])
        top_t[at, lanes] = jnp.broadcast_to(top, (TIME_ROWS, HD))
        sum_t[at, lanes] = jnp.broadcast_to(functools.reduce(jnp.add, exps), (TIME_ROWS, HD))
        acc_t[at, lanes] = acc

    def temporal_quarter(t, q):
        r0 = first_block(q, core) * BLK

        def body(i, _):
            r = pl.multiple_of(r0 + i * TIME_ROWS, TIME_ROWS)
            for h in range(heads):
                temporal(t, r, h)
            return 0

        lax.fori_loop(0, qrows // TIME_ROWS, body, 0)

    def attend(t, b):
        r = pl.ds(pl.multiple_of(b * BLK, BLK), BLK)
        live = counts[b]
        where, bias = [], []
        for j in range(MAXK):
            rel = pattern[b, j] - (space * blocks + b) + total_blocks // 2
            rel = jnp.bitwise_and(rel, total_blocks - 1) - total_blocks // 2
            where.append(jnp.clip(HALO + b + rel, 0, window - 1))
            bias.append(jnp.where(j < live, jnp.float32(0.0), jnp.float32(MASKED)))
        for h in range(heads):
            lanes = slice(h * HD, (h + 1) * HD)
            query = queries[r, lanes]
            scores = []
            for j in range(0, MAXK, 2):
                pair = jnp.concatenate([kv[t][where[j + i], 0, :, lanes] for i in range(2)], axis=0)
                s = lax.dot_general(
                    query, pair, (((1,), (1,)), ((), ())), preferred_element_type=F32
                )
                scores += [s[:, i * BLK : (i + 1) * BLK] + bias[j + i] for i in range(2)]
            top = jnp.max(functools.reduce(jnp.maximum, scores), axis=-1, keepdims=True)
            old = top_t[r, lanes]
            top = jnp.maximum(old, jnp.broadcast_to(top, (BLK, HD)))
            keep = jnp.exp2((old - top) * SCALE2)
            exps = [jnp.exp2((s - top) * SCALE2) for s in scores]
            total = jnp.sum(functools.reduce(jnp.add, exps), axis=-1, keepdims=True)
            acc = acc_t[r, lanes] * keep
            for j in range(0, MAXK, 2):
                pair = jnp.concatenate([kv[t][where[j + i], 1, :, lanes] for i in range(2)], axis=0)
                weights = jnp.concatenate([exps[j + i].astype(BF16) for i in range(2)], axis=1)
                acc = acc + jnp.dot(weights, pair, preferred_element_type=F32)
            total = sum_t[r, lanes] * keep + total
            out = pl.ds(pl.multiple_of(z * lw + h * HD, HD), HD)
            att[t, r, out] = (acc / total).astype(BF16)

    n_cols = 512

    def update(t, q):
        r = pl.ds(pl.multiple_of(first_block(q, core) * BLK, BLK), qrows)
        for n in range(0, width, n_cols):
            u = jnp.dot(att[t, r, :], wout[:, n : n + n_cols], preferred_element_type=F32)
            state[r, n : n + n_cols] = (state[r, n : n + n_cols].astype(F32) + u).astype(BF16)

    for i in range(NQ):
        in_copy(NQ - 1 - i).start()
    for copy in (weight_copies[1], weight_copies[2], weight_copies[0], w_out_copy):
        copy.start()
    for copy in cache_copies:
        copy.start()

    barrier = pltpu.get_barrier_semaphore()
    for dev in (up, down, partner, near_dev, far_dev, far_src):
        pl.semaphore_signal(barrier, inc=1, device_id=dev, device_id_type=MESH)
    pl.semaphore_wait(barrier, 6)

    weight_copies[1].wait()
    weight_copies[2].wait()
    weight_copies[0].wait()

    def first_qkv(i, _):
        q = NQ - 1 - i
        in_copy(q).wait()
        qkv(0, q)
        near_copy(0, q).start()
        chip_copy(0, q).start()
        qkv_queries(q)

        @pl.when(i == 0)
        def _():
            w_out_copy.wait()
            for d in range(2):
                w_copy(d).start()

        return 0

    lax.fori_loop(0, NQ, first_qkv, 0)
    for copy in cache_copies:
        copy.wait()

    def first_temporal(q, _):
        temporal_quarter(0, q)
        return 0

    lax.fori_loop(0, NQ, first_temporal, 0)

    for d in range(2):
        w_copy(d).wait_recv()
        w_forward(d).start()
    w_chip(0).start()
    w_chip(2).start()

    def near_wait(t):
        for q in (3, 2):
            near_copy(t, q).wait_recv()
            relay_copy(t, q).start()
        for q in (1, 0):
            near_copy(t, q).wait_recv()

    def far_wait(t):
        for q in range(2):
            far_copy(t, q).wait_recv()
        for i in range(4):
            kv[t][28 * core + i] = far[t, i]

    near_wait(0)
    for q in (0, 1):
        far_copy(0, q).start()
    for d in range(2):
        w_forward(d).wait_recv()
    w_chip(1).start()

    for t in range(STEPS):
        if t > 0:
            near_wait(t)
        for q in range(NQ):
            chip_copy(t, q).wait_recv()
        for q in (3, 2):
            relay_copy(t, q).wait_recv()

        def forward(t, q):
            for d in range(2):
                gather_copy(t, q, d).wait_recv()
                forward_copy(t, q, d).start()

        def attend_quarter(q, _, t=t):
            @pl.when(q == 2)
            def _():
                far_wait(t)

            b = first_block(q, core)

            def body(k, _):
                attend(t, b + k)
                return 0

            lax.fori_loop(0, QBLK, body, 0)
            for d in range(2):
                gather_copy(t, q, d).start()

            @pl.when(q > 0)
            def _():
                forward(t, q - 1)

            return 0

        lax.fori_loop(0, NQ, attend_quarter, 0)

        def finish_quarter(q, _, t=t):
            @pl.when(q == 0)
            def _():
                forward(t, NQ - 1)

            for d in range(2):
                forward_copy(t, q, d).wait_recv()
            if t == 0:

                @pl.when(q == 0)
                def _():
                    for k in range(3):
                        w_chip(k).wait_recv()

            update(t, q)
            if t + 1 < STEPS:
                qkv(t + 1, q)
                near_copy(t + 1, q).start()
                chip_copy(t + 1, q).start()

                @pl.when(q < 2)
                def _():
                    far_copy(t + 1, q).start()

                qkv_queries(q)
                temporal_quarter(t + 1, q)
            else:
                out_copy(q).start()
            return 0

        lax.fori_loop(0, NQ, finish_quarter, 0)

    for q in range(NQ):
        out_copy(q).wait()
    for t in range(STEPS):
        for q in range(NQ):
            near_copy(t, q).wait_send()
            chip_copy(t, q).wait_send()
            for d in range(2):
                gather_copy(t, q, d).wait_send()
                forward_copy(t, q, d).wait_send()
        for q in range(2):
            far_copy(t, q).wait_send()
            relay_copy(t, q + 2).wait_send()
    for d in range(2):
        w_copy(d).wait_send()
        w_forward(d).wait_send()
    for k in range(3):
        w_chip(k).wait_send()


def on_device(
    n_space, n_head,
    snapshot, norm_gain, w_query, w_key, w_value, w_out, cache_key, cache_value, pattern, counts,
):
    rows, width = snapshot.shape
    lw = w_query.shape[1]
    blocks = rows // BLK
    any_spec = pl.BlockSpec(memory_space=pl.ANY)
    smem = pl.BlockSpec(memory_space=pltpu.SMEM)
    window = blocks + 2 * HALO
    dma = pltpu.SemaphoreType.DMA
    return pl.pallas_call(
        functools.partial(kernel, n_space, n_head),
        out_shape=jax.ShapeDtypeStruct((rows, width), BF16),
        in_specs=[smem, smem, any_spec, pl.BlockSpec(memory_space=pltpu.VMEM)] + [any_spec] * 6,
        out_specs=any_spec,
        scratch_shapes=[
            pltpu.VMEM((rows, width), BF16),
            pltpu.VMEM((width, 3 * lw), BF16),
            pltpu.VMEM((width, width), BF16),
            pltpu.VMEM((FRAMES, rows, lw), BF16),
            pltpu.VMEM((FRAMES, rows, lw), BF16),
            pltpu.VMEM((window, 2, BLK, lw), BF16),
            pltpu.VMEM((window, 2, BLK, lw), BF16),
            pltpu.VMEM((STEPS, 4, 2, BLK, lw), BF16),
            pltpu.VMEM((STEPS, rows, width), BF16),
            pltpu.VMEM((rows, lw), BF16),
            pltpu.VMEM((QBLK * BLK, width), BF16),
            pltpu.VMEM((rows, lw), F32),
            pltpu.VMEM((rows, lw), F32),
            pltpu.VMEM((rows, lw), F32),
            dma((NQ,)), dma((4,)), dma((2,)), dma((NQ,)),
            dma((STEPS, NQ)), dma((STEPS, NQ)),
            dma((STEPS, NQ)), dma((STEPS, NQ)),
            dma((STEPS, 2)), dma((STEPS, 2)),
            dma((STEPS, 2)), dma((STEPS, 2)),
            dma((STEPS, NQ, 2)), dma((STEPS, NQ, 2)),
            dma((STEPS, NQ, 2)), dma((STEPS, NQ, 2)),
            dma((2,)), dma((2,)), dma((2,)), dma((2,)), dma((3,)), dma((3,)),
        ],
        compiler_params=pltpu.CompilerParams(
            collective_id=0, has_side_effects=True, vmem_limit_bytes=60 * 1024 * 1024
        ),
        name="rollout",
    )(
        pattern, counts, snapshot, norm_gain.reshape(1, width),
        w_query, w_key, w_value, w_out, cache_key, cache_value,
    )


def solution(mesh):
    placed = (
        P("space", None),
        P(),
        P(None, "head"),
        P(None, "head"),
        P(None, "head"),
        P("head", None),
        P(None, "space", "head"),
        P(None, "space", "head"),
        P("space", None),
        P("space"),
    )
    body = functools.partial(on_device, mesh.shape["space"], mesh.shape["head"])
    return jax.shard_map(
        body, mesh=mesh, in_specs=placed, out_specs=P("space", None), check_vma=False
    )
```

time: 433 us -> 135 us (0.31); the launches traced: 427 us -> 135 us
  waiting for transfers between devices: 190 us -> 0 us
  Pallas kernels: 0 us -> 130 us
  local copies, waits for them, and re-layouts: 108 us -> 5.05 us
  other arithmetic: 51.5 us -> 0 us
  matrix products: 46.7 us -> 0 us
  between operations: 15.8 us -> 0.01 us
  starting transfers between devices: 14.9 us -> 0 us
    psum x2 -> x0, waiting for transfers between devices: 154 us -> none  [on_device(): update = lax.psum(out_term.astype(jnp.bfloat16), 'head').astype(jnp.float32)]
    pallas_call x0 -> x1, Pallas kernels: none -> 130 us  [on_device(): pl.pallas_call(functools.partial(kernel, n_space, n_head), out_shape=jax....]
    unnamed x283 -> x1, local copies, waits for them, and re-layouts: 56.2 us -> 3.76 us
    dot_general x20 -> x0, matrix products: 46.7 us -> none  [the longest x6 12.5 us: on_device(): jnp.einsum('iwe,iea->iwa', spatial_attention_weight, per_head_value, pref...]
    ppermute x8 -> x0, waiting for transfers between devices: 36 us -> none  [shifted_2(): return lax.ppermute(value, axis, pairs)]
    gather x2 -> x0, local copies, waits for them, and re-layouts: 21.5 us -> none  [on_device(): jnp.take(window, where_block, axis=1)]
    slice x13 -> x0, local copies, waits for them, and re-layouts: 20.3 us -> none  [the longest x9 8.12 us: on_device(): value_frames[frame][:, :, low:high].astype(jnp.float32)]
    ppermute x8 -> x0, starting transfers between devices: 14.7 us -> none  [shifted_2(): return lax.ppermute(value, axis, pairs)]
  transfers between devices with their start and end apart: 10 -> 0, of which waited for: 5 -> 0; matrix products, arithmetic and copies ran while one was open for 21% -> 0% of each run, Pallas kernels for 0% -> 0%
where the time goes in v1:
time: 135 us
  Pallas kernels  130 us (96%)
  local copies, waits for them, and re-layouts  5.05 us (4%)
    pallas_call x1, Pallas kernels, on_device(): pl.pallas_call(functools.partial(kernel, n_space, n_head), out_shape=jax....  130 us
    unnamed x1, local copies, waits for them, and re-layouts  3.76 us

profile of v1, /device:TPU:1, one launch (start us, length us, event | category | flops | bytes accessed | tf_op | source)
XLA Modules:
  0.0 134.7 jit_solution(15480372562348497786)
XLA Ops:
  0.0 1.3 reshape.3.gain
  1.3 129.6 %rollout.1 = bf16[1024,1536]{1,0:T(8,128)(2,1)} custom-call(s32[8,8]{1,0:T(8,128)} %pattern.1, s32[8]{0:T(128)} %counts.1, bf16[1024,1536]{1,0:T(8,128)(2,1)} %snapshot.1, f32[1,1536]{1,0:T(1,128)} %reshape.3.gain, bf16[1536,384]{1,0:T(8,128)(2,1)} %w_query.1, bf16[1536,384]{1,0:T(8,128)(2,1)} %w_key.1, bf16[1536,384]{1,0:T(8,128)(2,1)} %w_value.1, ...), custom_call_target="tpu_custom_call" | custom-call | tf_op jit(solution)/shard_map/rollout/pallas_call | solution.py:421
  130.9 3.8 %copy.12 = bf16[1024,1536]{1,0:T(8,128)(2,1)} copy(bf16[1024,1536]{1,0:T(8,128)(2,1)} %rollout.1) | data formatting | bytes 6291456

commit v2 on v1

--- a/solution.py
+++ b/solution.py
@@ -22,16 +22,17 @@
 F32 = jnp.float32
 BF16 = jnp.bfloat16
 SCALE2 = math.log2(math.e) / math.sqrt(HD)
-NORM_ROWS = 32
+NORM_ROWS = 64
+COLS = 512
 TIME_ROWS = 32
 
 
 def kernel(
     n_space, n_head,
     pattern, counts, snapshot, gain, w_query, w_key, w_value, w_out, cache_key, cache_value,
-    rolled,
-    state, wqkv, wout, ckey, cvalue, kv0, kv1, far, att, queries, normed, top_t, sum_t, acc_t,
-    in_sem, w_sem, cache_sem, out_sem,
+    state,
+    wqkv, wout, ckey, cvalue, kv0, kv1, late, att, queries, normed, top_t, sum_t, acc_t,
+    in_sem, w_sem, cache_sem,
     near_s, near_r, chip_s, chip_r, far_s, far_r, rel_s, rel_r, ag_s, ag_r, fw_s, fw_r,
     wd_s, wd_r, wf_s, wf_r, wc_s, wc_r,
 ):
@@ -71,13 +72,25 @@
             src_ref=src, dst_ref=dst, send_sem=ssem, recv_sem=rsem, device_id=dev, device_id_type=MESH
         )
 
-    def near_copy(t, q):
+    def near_window(q):
+        return 4 + 16 * core + first_block(q, 1 - core)
+
+    def near_copy(t, q, last=False):
         b = first_block(q, core)
         return rcopy(
             kv[t].at[pl.ds(HALO + b, QBLK)],
-            kv[t].at[pl.ds(20 - 16 * core + b, QBLK)],
+            late.at[t, 0] if last else kv[t].at[pl.ds(20 - 16 * core + b, QBLK)],
             near_s.at[t, q], near_r.at[t, q], near_dev,
         )
+
+    def near_start(t, q):
+        @pl.when(q == 0)
+        def _():
+            near_copy(t, 0, True).start()
+
+        @pl.when(q > 0)
+        def _():
+            near_copy(t, q).start()
 
     def chip_copy(t, q):
         b = first_block(q, core)
@@ -91,12 +104,12 @@
         b = first_block(q, core)
         return rcopy(
             kv[t].at[pl.ds(HALO + b, QBLK)],
-            far.at[t, pl.ds(b - 4 * (1 - core), QBLK)],
+            late.at[t, 1 + q],
             far_s.at[t, q], far_r.at[t, q], far_dev,
         )
 
     def relay_copy(t, q):
-        w = 4 + 16 * core + first_block(q, 1 - core)
+        w = near_window(q)
         return rcopy(
             kv[t].at[pl.ds(w, QBLK)],
             kv[t].at[pl.ds(w - 8 + 16 * core, QBLK)],
@@ -136,15 +149,9 @@
             snapshot.at[pl.ds(r, qrows), :], state.at[pl.ds(r, qrows), :], in_sem.at[q]
         )
 
-    def out_copy(q):
-        r = pl.multiple_of(first_block(q, core) * BLK, BLK)
-        return pltpu.make_async_copy(
-            state.at[pl.ds(r, qrows), :], rolled.at[pl.ds(r, qrows), :], out_sem.at[q]
-        )
-
     weight_copies = [
         pltpu.make_async_copy(ref, wqkv.at[:, pl.ds(i * lw, lw)], w_sem.at[i])
-        for i, ref in enumerate((w_query, w_key, w_value))
+        for i, ref in enumerate((w_key, w_value, w_query))
     ]
     w_out_copy = pltpu.make_async_copy(w_out, w_rows(z, 0, lw), w_sem.at[3])
     cache_copies = [
@@ -161,24 +168,22 @@
             wide = state[pl.ds(r, NORM_ROWS), :].astype(F32)
             meansq = jnp.mean(wide * wide, axis=-1, keepdims=True)
             normed[pl.ds(pl.multiple_of(i * NORM_ROWS, NORM_ROWS), NORM_ROWS), :] = (
-                wide * lax.rsqrt(meansq + EPS) * gain[...]
+                wide * lax.rsqrt(meansq + EPS) * gain[...].reshape(1, width)
             ).astype(BF16)
             return 0
 
         lax.fori_loop(0, qrows // NORM_ROWS, norm_rows, 0)
-        for i in range(2):
-            out = jnp.dot(
-                normed[...], wqkv[:, lw * (1 + i) : lw * (2 + i)], preferred_element_type=F32
-            ).astype(BF16)
-            for k in range(QBLK):
-                kv[t][HALO + b + k, i] = out[k * BLK : (k + 1) * BLK]
-        return r0
-
-    def qkv_queries(q):
-        r0 = pl.multiple_of(first_block(q, core) * BLK, BLK)
-        queries[pl.ds(r0, qrows), :] = jnp.dot(
-            normed[...], wqkv[:, :lw], preferred_element_type=F32
-        ).astype(BF16)
+        for n in range(0, 3 * lw, COLS):
+            out = jnp.dot(normed[...], wqkv[:, n : n + COLS], preferred_element_type=F32)
+            for c in range(n, min(n + COLS, 3 * lw), HD):
+                kind, lane = divmod(c, lw)
+                piece = out[:, c - n : c - n + HD].astype(BF16)
+                lanes = slice(lane, lane + HD)
+                if kind == 2:
+                    queries[pl.ds(pl.multiple_of(r0, BLK), qrows), lanes] = piece
+                    continue
+                for k in range(QBLK):
+                    kv[t][HALO + b + k, kind, :, lanes] = piece[k * BLK : (k + 1) * BLK]
 
     def temporal(t, r, h):
         lanes = slice(h * HD, (h + 1) * HD)
@@ -244,88 +249,85 @@
             out = pl.ds(pl.multiple_of(z * lw + h * HD, HD), HD)
             att[t, r, out] = (acc / total).astype(BF16)
 
-    n_cols = 512
-
     def update(t, q):
         r = pl.ds(pl.multiple_of(first_block(q, core) * BLK, BLK), qrows)
-        for n in range(0, width, n_cols):
-            u = jnp.dot(att[t, r, :], wout[:, n : n + n_cols], preferred_element_type=F32)
-            state[r, n : n + n_cols] = (state[r, n : n + n_cols].astype(F32) + u).astype(BF16)
+        for n in range(0, width, COLS):
+            u = jnp.dot(att[t, r, :], wout[:, n : n + COLS], preferred_element_type=F32)
+            state[r, n : n + COLS] = (state[r, n : n + COLS].astype(F32) + u).astype(BF16)
 
     for i in range(NQ):
         in_copy(NQ - 1 - i).start()
-    for copy in (weight_copies[1], weight_copies[2], weight_copies[0], w_out_copy):
+    for copy in weight_copies:
         copy.start()
-    for copy in cache_copies:
-        copy.start()
+    w_out_copy.start()
 
     barrier = pltpu.get_barrier_semaphore()
     for dev in (up, down, partner, near_dev, far_dev, far_src):
         pl.semaphore_signal(barrier, inc=1, device_id=dev, device_id_type=MESH)
     pl.semaphore_wait(barrier, 6)
 
-    weight_copies[1].wait()
-    weight_copies[2].wait()
-    weight_copies[0].wait()
+    for copy in weight_copies:
+        copy.wait()
+    w_out_copy.wait()
+    for d in range(2):
+        w_copy(d).start()
+    for copy in cache_copies:
+        copy.start()
 
     def first_qkv(i, _):
         q = NQ - 1 - i
         in_copy(q).wait()
         qkv(0, q)
-        near_copy(0, q).start()
+        near_start(0, q)
         chip_copy(0, q).start()
-        qkv_queries(q)
-
-        @pl.when(i == 0)
-        def _():
-            w_out_copy.wait()
-            for d in range(2):
-                w_copy(d).start()
-
         return 0
 
     lax.fori_loop(0, NQ, first_qkv, 0)
     for copy in cache_copies:
         copy.wait()
 
+    def near_wait(t, q):
+        near_copy(t, q).wait_recv()
+        if q >= 2:
+            relay_copy(t, q).start()
+
+    def land(t, slot, w):
+        for i in range(QBLK):
+            kv[t][w + i] = late[t, slot, i]
+
+    def far_land(t, q):
+        far_copy(t, q).wait_recv()
+        b = first_block(q, core)
+        land(t, 1 + q, 28 * core + b - 4 * (1 - core))
+
     def first_temporal(q, _):
         temporal_quarter(0, q)
+
+        @pl.when(q == 2)
+        def _():
+            for d in range(2):
+                w_copy(d).wait_recv()
+                w_forward(d).start()
+            w_chip(0).start()
+            w_chip(2).start()
+            for k in (3, 2):
+                near_wait(0, k)
+
         return 0
 
     lax.fori_loop(0, NQ, first_temporal, 0)
 
-    for d in range(2):
-        w_copy(d).wait_recv()
-        w_forward(d).start()
-    w_chip(0).start()
-    w_chip(2).start()
-
-    def near_wait(t):
-        for q in (3, 2):
-            near_copy(t, q).wait_recv()
-            relay_copy(t, q).start()
-        for q in (1, 0):
-            near_copy(t, q).wait_recv()
-
-    def far_wait(t):
-        for q in range(2):
-            far_copy(t, q).wait_recv()
-        for i in range(4):
-            kv[t][28 * core + i] = far[t, i]
-
-    near_wait(0)
-    for q in (0, 1):
-        far_copy(0, q).start()
-    for d in range(2):
-        w_forward(d).wait_recv()
-    w_chip(1).start()
-
     for t in range(STEPS):
-        if t > 0:
-            near_wait(t)
+        if t == 0:
+            near_wait(t, 1)
+            far_copy(t, 0).start()
+        else:
+            for q in (1, 2, 3):
+                near_wait(t, q)
+            far_copy(t, 1).start()
         for q in range(NQ):
             chip_copy(t, q).wait_recv()
-        for q in (3, 2):
+        for q in (2, 3):
             relay_copy(t, q).wait_recv()
 
         def forward(t, q):
@@ -334,9 +336,17 @@
                 forward_copy(t, q, d).start()
 
         def attend_quarter(q, _, t=t):
-            @pl.when(q == 2)
+            @pl.when(q == 1)
             def _():
-                far_wait(t)
+                near_copy(t, 0, True).wait_recv()
+                if t == 0:
+                    far_copy(t, 1).start()
+                land(t, 0, near_window(0))
+
+            @pl.when(q > 1)
+            def _():
+                forward(t, q - 2)
+                far_land(t, q - 2)
 
             b = first_block(q, core)
 
@@ -348,18 +358,22 @@
             for d in range(2):
                 gather_copy(t, q, d).start()
 
-            @pl.when(q > 0)
+            if t == 0:
+
+                @pl.when(q == 2)
+                def _():
+                    for d in range(2):
+                        w_forward(d).wait_recv()
+                    w_chip(1).start()
+
+            return 0
+
+        lax.fori_loop(0, NQ, attend_quarter, 0)
+
+        def finish_quarter(q, _, t=t):
+            @pl.when((q == 1) | (q == 2))
             def _():
-                forward(t, q - 1)
-
-            return 0
-
-        lax.fori_loop(0, NQ, attend_quarter, 0)
-
-        def finish_quarter(q, _, t=t):
-            @pl.when(q == 0)
-            def _():
-                forward(t, NQ - 1)
+                forward(t, q + 1)
 
             for d in range(2):
                 forward_copy(t, q, d).wait_recv()
@@ -373,26 +387,21 @@
             update(t, q)
             if t + 1 < STEPS:
                 qkv(t + 1, q)
-                near_copy(t + 1, q).start()
+                near_start(t + 1, q)
                 chip_copy(t + 1, q).start()
 
-                @pl.when(q < 2)
+                @pl.when(q == 0)
                 def _():
-                    far_copy(t + 1, q).start()
-
-                qkv_queries(q)
+                    far_copy(t + 1, 0).start()
+
                 temporal_quarter(t + 1, q)
-            else:
-                out_copy(q).start()
             return 0
 
         lax.fori_loop(0, NQ, finish_quarter, 0)
 
-    for q in range(NQ):
-        out_copy(q).wait()
     for t in range(STEPS):
         for q in range(NQ):
-            near_copy(t, q).wait_send()
+            near_copy(t, q, q == 0).wait_send()
             chip_copy(t, q).wait_send()
             for d in range(2):
                 gather_copy(t, q, d).wait_send()
@@ -420,25 +429,24 @@
     dma = pltpu.SemaphoreType.DMA
     return pl.pallas_call(
         functools.partial(kernel, n_space, n_head),
-        out_shape=jax.ShapeDtypeStruct((rows, width), BF16),
+        out_shape=pltpu.VMEM((rows, width), BF16),
         in_specs=[smem, smem, any_spec, pl.BlockSpec(memory_space=pltpu.VMEM)] + [any_spec] * 6,
-        out_specs=any_spec,
+        out_specs=pl.BlockSpec(memory_space=pltpu.VMEM),
         scratch_shapes=[
-            pltpu.VMEM((rows, width), BF16),
             pltpu.VMEM((width, 3 * lw), BF16),
             pltpu.VMEM((width, width), BF16),
             pltpu.VMEM((FRAMES, rows, lw), BF16),
             pltpu.VMEM((FRAMES, rows, lw), BF16),
             pltpu.VMEM((window, 2, BLK, lw), BF16),
             pltpu.VMEM((window, 2, BLK, lw), BF16),
-            pltpu.VMEM((STEPS, 4, 2, BLK, lw), BF16),
+            pltpu.VMEM((STEPS, 3, QBLK, 2, BLK, lw), BF16),
             pltpu.VMEM((STEPS, rows, width), BF16),
             pltpu.VMEM((rows, lw), BF16),
             pltpu.VMEM((QBLK * BLK, width), BF16),
             pltpu.VMEM((rows, lw), F32),
             pltpu.VMEM((rows, lw), F32),
             pltpu.VMEM((rows, lw), F32),
-            dma((NQ,)), dma((4,)), dma((2,)), dma((NQ,)),
+            dma((NQ,)), dma((4,)), dma((2,)),
             dma((STEPS, NQ)), dma((STEPS, NQ)),
             dma((STEPS, NQ)), dma((STEPS, NQ)),
             dma((STEPS, 2)), dma((STEPS, 2)),
@@ -448,11 +456,11 @@
             dma((2,)), dma((2,)), dma((2,)), dma((2,)), dma((3,)), dma((3,)),
         ],
         compiler_params=pltpu.CompilerParams(
-            collective_id=0, has_side_effects=True, vmem_limit_bytes=60 * 1024 * 1024
+            collective_id=0, has_side_effects=True, vmem_limit_bytes=56 * 1024 * 1024
         ),
         name="rollout",
     )(
-        pattern, counts, snapshot, norm_gain.reshape(1, width),
+        pattern, counts, snapshot, norm_gain,
         w_query, w_key, w_value, w_out, cache_key, cache_value,
     )
 

time: 135 us -> 108 us (0.80)
  Pallas kernels: 130 us -> 106 us
  local copies, waits for them, and re-layouts: 5.05 us -> 1.67 us
    pallas_call x1, Pallas kernels: 130 us -> 106 us  [on_device(): pl.pallas_call(functools.partial(kernel, n_space, n_head), out_shape=pltp...]
    unnamed x1, local copies, waits for them, and re-layouts: 3.76 us -> 1.67 us
where the time goes in v2:
time: 108 us
  Pallas kernels  106 us (98%)
  local copies, waits for them, and re-layouts  1.67 us (2%)
    pallas_call x1, Pallas kernels, on_device(): pl.pallas_call(functools.partial(kernel, n_space, n_head), out_shape=pltp...  106 us

profile of v2, /device:TPU:1, one launch (start us, length us, event | category | flops | bytes accessed | tf_op | source)
XLA Modules:
  0.0 107.8 jit_solution(12131265626618096855)
XLA Ops:
  0.0 106.1 %rollout.1 = bf16[1024,1536]{1,0:T(8,128)(2,1)S(1)} custom-call(s32[8,8]{1,0:T(8,128)} %pattern.1, s32[8]{0:T(128)} %counts.1, bf16[1024,1536]{1,0:T(8,128)(2,1)} %snapshot.1, f32[1536]{0:T(1024)} %gain.1, bf16[1536,384]{1,0:T(8,128)(2,1)} %w_query.1, bf16[1536,384]{1,0:T(8,128)(2,1)} %w_key.1, bf16[1536,384]{1,0:T(8,128)(2,1)} %w_value.1, ...), custom_call_target="tpu_custom_call" | custom-call | tf_op jit(solution)/shard_map/rollout/pallas_call | solution.py:430
  106.1 1.7 %copy.12 = bf16[1024,1536]{1,0:T(8,128)(2,1)} copy(bf16[1024,1536]{1,0:T(8,128)(2,1)S(1)} %rollout.1) | data formatting | bytes 6291456

commit v3 on v2

v3 whole, which is shorter than its diff:
```python
import functools
import math

import jax
import jax.numpy as jnp
from jax import lax
from jax.experimental import pallas as pl
from jax.experimental.pallas import tpu as pltpu
from jax.sharding import PartitionSpec as P

HD = 128
BLK = 128
MAXK = 8
FRAMES = 8
STEPS = 2
HALO = 12
FAR = 4
FORWARD_LAG = (2, 2)
FINISH_LAG = (4, 4)
NEAR_LATE = 3
EPS = 1e-05
MASKED = -1e30
MESH = pl.DeviceIdType.MESH
F32 = jnp.float32
BF16 = jnp.bfloat16
SCALE2 = math.log2(math.e) / math.sqrt(HD)
NORM_ROWS = 64
COLS = 512
TIME_ROWS = 32


def kernel(
    n_space, n_head,
    pattern, counts, snapshot, gain, w_query, w_key, w_value, w_out, cache_key, cache_value,
    state,
    wqkv, wout, ckey, cvalue, kv0, kv1, late, att, queries, normed, top_t, sum_t, acc_t, scores, weights,
    in_sem, w_sem, cache_sem,
    near_s, near_r, chip_s, chip_r, far_s, far_r, rel_s, rel_r, ag_s, ag_r, fw_s, fw_r,
    wd_s, wd_r, wf_s, wf_r, wc_s, wc_r,
):
    kv = (kv0, kv1)
    rows, width = state.shape
    lw = w_query.shape[1]
    heads = lw // HD
    blocks = rows // BLK
    total_blocks = blocks * n_space
    window = kv0.shape[0]

    space = lax.axis_index("space")
    z = lax.axis_index("head")
    core = lax.rem(space, 2)

    def wrap(s):
        return lax.rem(s + n_space, n_space)

    up = (space, lax.rem(z + 1, n_head))
    down = (space, lax.rem(z + n_head - 1, n_head))
    partner = (space + 1 - 2 * core, z)
    near_dev = (wrap(space - 1 + 2 * core), z)
    far_dev = (wrap(space + 2 - 4 * core), z)
    far_src = (wrap(space - 2 + 4 * core), z)
    z_up = lax.rem(z + 1, n_head)
    z_down = lax.rem(z + n_head - 1, n_head)

    def block_of(q, c):
        return (1 - c) * (blocks - 1 - q) + c * q

    def rcopy(src, dst, ssem, rsem, dev):
        return pltpu.make_async_remote_copy(
            src_ref=src, dst_ref=dst, send_sem=ssem, recv_sem=rsem, device_id=dev, device_id_type=MESH
        )

    def near_window(q):
        return 4 + 16 * core + block_of(q, 1 - core)

    def near_copy(t, q, last=False):
        b = block_of(q, core)
        return rcopy(
            kv[t].at[HALO + b],
            late.at[t, NEAR_LATE - 1 - q] if last else kv[t].at[20 - 16 * core + b],
            near_s.at[t, q], near_r.at[t, q], near_dev,
        )

    def near_start(t, q):
        @pl.when(q < NEAR_LATE)
        def _():
            near_copy(t, q, True).start()

        @pl.when(q >= NEAR_LATE)
        def _():
            near_copy(t, q).start()

    def chip_copy(t, q):
        b = block_of(q, core)
        return rcopy(
            kv[t].at[HALO + b],
            kv[t].at[4 + 16 * core + b],
            chip_s.at[t, q], chip_r.at[t, q], partner,
        )

    def far_copy(t, q):
        b = block_of(q, core)
        return rcopy(
            kv[t].at[HALO + b],
            late.at[t, NEAR_LATE + q],
            far_s.at[t, q], far_r.at[t, q], far_dev,
        )

    def relay_copy(t, q):
        w = near_window(q)
        return rcopy(
            kv[t].at[w],
            kv[t].at[w - 8 + 16 * core],
            rel_s.at[t, q - FAR], rel_r.at[t, q - FAR], partner,
        )

    def gather_copy(t, q, d):
        r = pl.multiple_of(block_of(q, core) * BLK, BLK)
        part = att.at[t, pl.ds(z * heads, heads), pl.ds(r, BLK), :]
        return rcopy(part, part, ag_s.at[t, q, d], ag_r.at[t, q, d], up if d == 0 else down)

    def forward_copy(t, q, d):
        r = pl.multiple_of(block_of(q, core) * BLK + d * (BLK // 2), BLK // 2)
        source = z_down if d == 0 else z_up
        part = att.at[t, pl.ds(source * heads, heads), pl.ds(r, BLK // 2), :]
        return rcopy(part, part, fw_s.at[t, q, d], fw_r.at[t, q, d], up if d == 0 else down)

    half = lw // 2

    def w_rows(group, offset, count):
        return wout.at[pl.ds(pl.multiple_of(group * lw + offset, 32), count), :]

    def w_copy(d):
        part = w_rows(z, half * core, half)
        return rcopy(part, part, wd_s.at[d], wd_r.at[d], up if d == 0 else down)

    def w_forward(d):
        part = w_rows(z_down if d == 0 else z_up, half * core + d * (half // 2), half // 2)
        return rcopy(part, part, wf_s.at[d], wf_r.at[d], up if d == 0 else down)

    def w_chip(k):
        part = w_rows(lax.rem(z + 1 + k, n_head), half * core, half)
        return rcopy(part, part, wc_s.at[k], wc_r.at[k], partner)

    def in_copy(q):
        r = pl.multiple_of(block_of(q, core) * BLK, BLK)
        return pltpu.make_async_copy(
            snapshot.at[pl.ds(r, BLK), :], state.at[pl.ds(r, BLK), :], in_sem.at[q]
        )

    weight_copies = [
        pltpu.make_async_copy(ref, wqkv.at[:, pl.ds(i * lw, lw)], w_sem.at[i])
        for i, ref in enumerate((w_key, w_value, w_query))
    ]
    w_out_copy = pltpu.make_async_copy(w_out, w_rows(z, 0, lw), w_sem.at[3])
    cache_copies = [
        pltpu.make_async_copy(cache_key, ckey, cache_sem.at[0]),
        pltpu.make_async_copy(cache_value, cvalue, cache_sem.at[1]),
    ]

    def qkv(t, q):
        b = block_of(q, core)
        r0 = b * BLK

        def norm_rows(i, _):
            r = pl.multiple_of(r0 + i * NORM_ROWS, NORM_ROWS)
            wide = state[pl.ds(r, NORM_ROWS), :].astype(F32)
            meansq = jnp.mean(wide * wide, axis=-1, keepdims=True)
            normed[pl.ds(pl.multiple_of(i * NORM_ROWS, NORM_ROWS), NORM_ROWS), :] = (
                wide * lax.rsqrt(meansq + EPS) * gain[...].reshape(1, width)
            ).astype(BF16)
            return 0

        lax.fori_loop(0, BLK // NORM_ROWS, norm_rows, 0)
        for n in range(0, 3 * lw, COLS):
            out = jnp.dot(normed[...], wqkv[:, n : n + COLS], preferred_element_type=F32)
            for c in range(n, min(n + COLS, 3 * lw), HD):
                kind, lane = divmod(c, lw)
                piece = out[:, c - n : c - n + HD].astype(BF16)
                if kind == 2:
                    queries[lane // HD, pl.ds(pl.multiple_of(r0, BLK), BLK), :] = piece
                    continue
                kv[t][HALO + b, kind, lane // HD] = piece

    def temporal(t, r, h):
        lanes = slice(h * HD, (h + 1) * HD)
        at = pl.ds(r, TIME_ROWS)
        query = queries[h, at, :].astype(F32)
        b = lax.div(r, BLK)
        inner = pl.ds(pl.multiple_of(lax.rem(r, BLK), TIME_ROWS), TIME_ROWS)
        frames = range(t, FRAMES)
        keys = [ckey[f, at, lanes] for f in frames]
        keys += [kv0[HALO + b, 0, h, inner]] * t
        scores = [jnp.sum(query * k.astype(F32), axis=-1, keepdims=True) for k in keys]
        top = functools.reduce(jnp.maximum, scores)
        exps = [jnp.exp2((s - top) * SCALE2) for s in scores]
        values = [cvalue[f, at, lanes] for f in frames]
        values += [kv0[HALO + b, 1, h, inner]] * t
        acc = functools.reduce(jnp.add, [e * v.astype(F32) for e, v in zip(exps, values)])
        top_t[at, lanes] = jnp.broadcast_to(top, (TIME_ROWS, HD))
        sum_t[at, lanes] = jnp.broadcast_to(functools.reduce(jnp.add, exps), (TIME_ROWS, HD))
        acc_t[at, lanes] = acc

    def temporal_block(t, q):
        r0 = block_of(q, core) * BLK

        def body(i, _):
            r = pl.multiple_of(r0 + i * TIME_ROWS, TIME_ROWS)
            for h in range(heads):
                temporal(t, r, h)
            return 0

        lax.fori_loop(0, BLK // TIME_ROWS, body, 0)

    def attend(t, b):
        r = pl.ds(pl.multiple_of(b * BLK, BLK), BLK)
        live = counts[b]
        where, bias = [], []
        for j in range(MAXK):
            rel = pattern[b, j] - (space * blocks + b) + total_blocks // 2
            rel = jnp.bitwise_and(rel, total_blocks - 1) - total_blocks // 2
            where.append(jnp.clip(HALO + b + rel, 0, window - 1))
            bias.append(jnp.where(j < live, jnp.float32(0.0), jnp.float32(MASKED)))
        tops = []
        for h in range(heads):
            lanes = slice(h * HD, (h + 1) * HD)
            query = queries[h, r, :]
            top = None
            for j in range(0, MAXK, 2):
                pair = jnp.concatenate([kv[t][where[j + i], 0, h] for i in range(2)], axis=0)
                s = lax.dot_general(
                    query, pair, (((1,), (1,)), ((), ())), preferred_element_type=F32
                )
                for i in range(2):
                    slot = s[:, i * BLK : (i + 1) * BLK] + bias[j + i]
                    scores[h, j + i] = slot
                    top = slot if top is None else jnp.maximum(top, slot)
            tops.append(jnp.max(top, axis=-1, keepdims=True))
        for h in range(heads):
            lanes = slice(h * HD, (h + 1) * HD)
            old = top_t[r, lanes]
            top = jnp.maximum(old, jnp.broadcast_to(tops[h], (BLK, HD)))
            keep = jnp.exp2((old - top) * SCALE2)
            total = None
            for j in range(MAXK):
                e = jnp.exp2((scores[h, j] - top) * SCALE2)
                weights[h, j] = e.astype(BF16)
                total = e if total is None else total + e
            total = sum_t[r, lanes] * keep + jnp.sum(total, axis=-1, keepdims=True)
            values = jnp.concatenate([kv[t][where[j], 1, h] for j in range(MAXK)], axis=0)
            probs = jnp.concatenate([weights[h, j] for j in range(MAXK)], axis=1)
            mixed = jnp.dot(probs, values, preferred_element_type=F32)
            att[t, z * heads + h, r, :] = ((acc_t[r, lanes] * keep + mixed) / total).astype(BF16)

    def update(t, q):
        r = pl.ds(pl.multiple_of(block_of(q, core) * BLK, BLK), BLK)
        mixed = jnp.concatenate([att[t, i, r, :] for i in range(width // HD)], axis=1)
        for n in range(0, width, COLS):
            u = jnp.dot(mixed, wout[:, n : n + COLS], preferred_element_type=F32)
            state[r, n : n + COLS] = (state[r, n : n + COLS].astype(F32) + u).astype(BF16)

    for q in reversed(range(blocks)):
        in_copy(q).start()
    for copy in weight_copies:
        copy.start()
    w_out_copy.start()

    barrier = pltpu.get_barrier_semaphore()
    for dev in (up, down, partner, near_dev, far_dev, far_src):
        pl.semaphore_signal(barrier, inc=1, device_id=dev, device_id_type=MESH)
    pl.semaphore_wait(barrier, 6)

    for copy in weight_copies:
        copy.wait()
    w_out_copy.wait()
    for d in range(2):
        w_copy(d).start()
    for copy in cache_copies:
        copy.start()

    def first_qkv(i, _):
        q = blocks - 1 - i
        in_copy(q).wait()
        qkv(0, q)
        near_start(0, q)
        chip_copy(0, q).start()
        return 0

    lax.fori_loop(0, blocks, first_qkv, 0)
    for copy in cache_copies:
        copy.wait()

    def near_wait(t, q):
        near_copy(t, q).wait_recv()
        relay_copy(t, q).start()

    early = (5, 1)

    def first_temporal(q, _):
        temporal_block(0, q)

        @pl.when(q > 0)
        def _():
            near_wait(0, blocks - q)

        return 0

    lax.fori_loop(0, early[0], first_temporal, 0)

    def forward(t, q):
        for d in range(2):
            gather_copy(t, q, d).wait_recv()
            forward_copy(t, q, d).start()

    def land_near(t, q):
        near_copy(t, q, True).wait_recv()
        kv[t][near_window(q)] = late[t, NEAR_LATE - 1 - q]

    def land_far(t, q):
        far_copy(t, q).wait_recv()
        kv[t][28 * core + block_of(q, core) - FAR * (1 - core)] = late[t, NEAR_LATE + q]

    for t in range(STEPS):
        last = t + 1 == STEPS
        if t == 0:
            near_copy(t, 3).wait_recv()
            far_copy(t, 0).start()
            for d in range(2):
                w_copy(d).wait_recv()
                w_forward(d).start()
            w_chip(0).start()
            w_chip(2).start()
        else:
            near_copy(t, 3).wait_recv()
            for q in (4, 5, 6):
                near_wait(t, q)
            temporal_block(t, 0)
            near_wait(t, 7)
            far_copy(t, 2).start()
            far_copy(t, 3).start()
        for q in range(blocks):
            chip_copy(t, q).wait_recv()
        for q in range(FAR, blocks):
            relay_copy(t, q).wait_recv()

        def tick(i, _, t=t, last=last):
            @pl.when(i < blocks)
            def _():
                @pl.when((i > 0) & (i <= NEAR_LATE))
                def _():
                    land_near(t, NEAR_LATE - i)
                    if t == 0:
                        far_copy(t, i).start()

                @pl.when(i > NEAR_LATE)
                def _():
                    land_far(t, i - NEAR_LATE - 1)

                attend(t, block_of(i, core))
                for d in range(2):
                    gather_copy(t, i, d).start()

            @pl.when((i >= FORWARD_LAG[t]) & (i < blocks + FORWARD_LAG[t]))
            def _():
                forward(t, i - FORWARD_LAG[t])

            @pl.when(i < blocks - early[t])
            def _():
                temporal_block(t, i + early[t])

            if t == 0:

                @pl.when(i == FINISH_LAG[t])
                def _():
                    for d in range(2):
                        w_forward(d).wait_recv()
                    w_chip(1).start()
                    for k in range(3):
                        w_chip(k).wait_recv()

            @pl.when(i >= FINISH_LAG[t])
            def _():
                q = i - FINISH_LAG[t]
                for d in range(2):
                    forward_copy(t, q, d).wait_recv()
                update(t, q)
                if not last:
                    qkv(t + 1, q)
                    near_start(t + 1, q)
                    chip_copy(t + 1, q).start()

                    @pl.when(q < 2)
                    def _():
                        far_copy(t + 1, q).start()

            return 0

        lax.fori_loop(0, blocks + FINISH_LAG[t], tick, 0)

    for t in range(STEPS):

        def drain(q, _, t=t):
            @pl.when(q < NEAR_LATE)
            def _():
                near_copy(t, q, True).wait_send()

            @pl.when(q >= NEAR_LATE)
            def _():
                near_copy(t, q).wait_send()

            chip_copy(t, q).wait_send()
            for d in range(2):
                gather_copy(t, q, d).wait_send()
                forward_copy(t, q, d).wait_send()

            @pl.when(q < FAR)
            def _():
                far_copy(t, q).wait_send()

            @pl.when(q >= FAR)
            def _():
                relay_copy(t, q).wait_send()

            return 0

        lax.fori_loop(0, blocks, drain, 0)
    for d in range(2):
        w_copy(d).wait_send()
        w_forward(d).wait_send()
    for k in range(3):
        w_chip(k).wait_send()


def on_device(
    n_space, n_head,
    snapshot, norm_gain, w_query, w_key, w_value, w_out, cache_key, cache_value, pattern, counts,
):
    rows, width = snapshot.shape
    lw = w_query.shape[1]
    blocks = rows // BLK
    heads = lw // HD
    any_spec = pl.BlockSpec(memory_space=pl.ANY)
    smem = pl.BlockSpec(memory_space=pltpu.SMEM)
    window = blocks + 2 * HALO
    dma = pltpu.SemaphoreType.DMA
    return pl.pallas_call(
        functools.partial(kernel, n_space, n_head),
        out_shape=pltpu.VMEM((rows, width), BF16),
        in_specs=[smem, smem, any_spec, pl.BlockSpec(memory_space=pltpu.VMEM)] + [any_spec] * 6,
        out_specs=pl.BlockSpec(memory_space=pltpu.VMEM),
        scratch_shapes=[
            pltpu.VMEM((width, 3 * lw), BF16),
            pltpu.VMEM((width, width), BF16),
            pltpu.VMEM((FRAMES, rows, lw), BF16),
            pltpu.VMEM((FRAMES, rows, lw), BF16),
            pltpu.VMEM((window, 2, heads, BLK, HD), BF16),
            pltpu.VMEM((window, 2, heads, BLK, HD), BF16),
            pltpu.VMEM((STEPS, NEAR_LATE + FAR, 2, heads, BLK, HD), BF16),
            pltpu.VMEM((STEPS, width // HD, rows, HD), BF16),
            pltpu.VMEM((heads, rows, HD), BF16),
            pltpu.VMEM((BLK, width), BF16),
            pltpu.VMEM((rows, lw), F32),
            pltpu.VMEM((rows, lw), F32),
            pltpu.VMEM((rows, lw), F32),
            pltpu.VMEM((heads, MAXK, BLK, BLK), F32),
            pltpu.VMEM((heads, MAXK, BLK, BLK), BF16),
            dma((blocks,)), dma((4,)), dma((2,)),
            dma((STEPS, blocks)), dma((STEPS, blocks)),
            dma((STEPS, blocks)), dma((STEPS, blocks)),
            dma((STEPS, FAR)), dma((STEPS, FAR)),
            dma((STEPS, FAR)), dma((STEPS, FAR)),
            dma((STEPS, blocks, 2)), dma((STEPS, blocks, 2)),
            dma((STEPS, blocks, 2)), dma((STEPS, blocks, 2)),
            dma((2,)), dma((2,)), dma((2,)), dma((2,)), dma((3,)), dma((3,)),
        ],
        compiler_params=pltpu.CompilerParams(
            collective_id=0, has_side_effects=True, vmem_limit_bytes=56 * 1024 * 1024
        ),
        name="rollout",
    )(
        pattern, counts, snapshot, norm_gain,
        w_query, w_key, w_value, w_out, cache_key, cache_value,
    )


def solution(mesh):
    placed = (
        P("space", None),
        P(),
        P(None, "head"),
        P(None, "head"),
        P(None, "head"),
        P("head", None),
        P(None, "space", "head"),
        P(None, "space", "head"),
        P("space", None),
        P("space"),
    )
    body = functools.partial(on_device, mesh.shape["space"], mesh.shape["head"])
    return jax.shard_map(
        body, mesh=mesh, in_specs=placed, out_specs=P("space", None), check_vma=False
    )
```

time: 108 us -> 102 us (0.944)
  Pallas kernels: 106 us -> 100 us
    pallas_call x1, Pallas kernels: 106 us -> 100 us  [on_device(): pl.pallas_call(functools.partial(kernel, n_space, n_head), out_shape=pltp...]
where the time goes in v3:
time: 102 us
  Pallas kernels  100 us (98%)
  local copies, waits for them, and re-layouts  1.67 us (2%)
    pallas_call x1, Pallas kernels, on_device(): pl.pallas_call(functools.partial(kernel, n_space, n_head), out_shape=pltp...  100 us

profile of v3, /device:TPU:1, one launch (start us, length us, event | category | flops | bytes accessed | tf_op | source)
XLA Modules:
  0.0 102.1 jit_solution(2114233546491216076)
XLA Ops:
  0.0 100.4 %rollout.1 = bf16[1024,1536]{1,0:T(8,128)(2,1)S(1)} custom-call(s32[8,8]{1,0:T(8,128)} %pattern.1, s32[8]{0:T(128)} %counts.1, bf16[1024,1536]{1,0:T(8,128)(2,1)} %snapshot.1, f32[1536]{0:T(1024)} %gain.1, bf16[1536,384]{1,0:T(8,128)(2,1)} %w_query.1, bf16[1536,384]{1,0:T(8,128)(2,1)} %w_key.1, bf16[1536,384]{1,0:T(8,128)(2,1)} %w_value.1, ...), custom_call_target="tpu_custom_call" | custom-call | tf_op jit(solution)/shard_map/rollout/pallas_call | solution.py:446
  100.4 1.7 %copy.12 = bf16[1024,1536]{1,0:T(8,128)(2,1)} copy(bf16[1024,1536]{1,0:T(8,128)(2,1)S(1)} %rollout.1) | data formatting | bytes 6291456

commit v4 on v3

--- a/solution.py
+++ b/solution.py
@@ -336,8 +336,8 @@
                 near_wait(t, q)
             temporal_block(t, 0)
             near_wait(t, 7)
-            far_copy(t, 2).start()
-            far_copy(t, 3).start()
+            for q in range(FAR):
+                far_copy(t, q).start()
         for q in range(blocks):
             chip_copy(t, q).wait_recv()
         for q in range(FAR, blocks):
@@ -388,10 +388,6 @@
                     qkv(t + 1, q)
                     near_start(t + 1, q)
                     chip_copy(t + 1, q).start()
-
-                    @pl.when(q < 2)
-                    def _():
-                        far_copy(t + 1, q).start()
 
             return 0
 

time: 102 us -> 102 us (level)
  no operation moved by 1% of the time
where the time goes in v4:
time: 102 us
  Pallas kernels  100 us (98%)
  local copies, waits for them, and re-layouts  1.67 us (2%)
    pallas_call x1, Pallas kernels, on_device(): pl.pallas_call(functools.partial(kernel, n_space, n_head), out_shape=pltp...  100 us

profile of v4, /device:TPU:1, one launch (start us, length us, event | category | flops | bytes accessed | tf_op | source)
XLA Modules:
  0.0 102.0 jit_solution(13822836255542505038)
XLA Ops:
  0.0 100.3 %rollout.1 = bf16[1024,1536]{1,0:T(8,128)(2,1)S(1)} custom-call(s32[8,8]{1,0:T(8,128)} %pattern.1, s32[8]{0:T(128)} %counts.1, bf16[1024,1536]{1,0:T(8,128)(2,1)} %snapshot.1, f32[1536]{0:T(1024)} %gain.1, bf16[1536,384]{1,0:T(8,128)(2,1)} %w_query.1, bf16[1536,384]{1,0:T(8,128)(2,1)} %w_key.1, bf16[1536,384]{1,0:T(8,128)(2,1)} %w_value.1, ...), custom_call_target="tpu_custom_call" | custom-call | tf_op jit(solution)/shard_map/rollout/pallas_call | solution.py:442
  100.3 1.7 %copy.12 = bf16[1024,1536]{1,0:T(8,128)(2,1)} copy(bf16[1024,1536]{1,0:T(8,128)(2,1)S(1)} %rollout.1) | data formatting | bytes 6291456
